TPU v7x, 32 devices: a whole 2x2x4 slice. The times are simulated.
32 devices in a mesh: leaf: 8 (over z, y), row: 4 (over x, core).
Axes of the slice: x: 2, y: 2, z: 4, core: 2. Of those that a mesh axis runs over, the one named last changes fastest.
Arguments:
- panel0: float32 [12288, 512], P(('leaf', 'row')), may hold values from -3 to 30, as said below
- panel1: float32 [6144, 512], P(('leaf', 'row')), may hold values from -3 to 30
- panel2: float32 [3072, 512], P(('leaf', 'row')), may hold values from -3 to 30
- panel3: float32 [1536, 512], P(('leaf', 'row')), may hold values from -3 to 30
- maps1: int32 [8, 8], replicated, may hold values from 0 to 11, as said below
- maps2: int32 [4, 8], replicated, may hold values from 0 to 11, as said below
- maps3: int32 [2, 8], replicated, may hold values from 0 to 11, as said below
Outputs:
- update_top: float32 [1024, 1024], P(('leaf', 'row'))
Inputs may be any that keep to these rules, and one draw needn't show every extreme that they name: `panel0`: each front's first 512 rows form a symmetric matrix, and every assembled pivot block is positive definite. `maps1`: each row lists distinct parent block numbers. `maps2`: each row lists distinct parent block numbers. `maps3`: each row lists distinct parent block numbers.
All inputs are finite; a program needn't handle non-finite values.
Results may differ from a plain program's by a relative error of at most 0.0003.
Values sent between devices are 32-bit elements; how exact they have to be, the bound alone decides.
A program may use at most 128 MiB of HBM per device.

v0:
```python
import jax
import jax.numpy as jnp
from jax import lax
from jax.sharding import PartitionSpec as P

BLOCK = 128
PIV = 512
UPD = 1024


exact_mode = lax.Precision.HIGHEST


def partner(block, axis, stride):
    count = lax.axis_size(axis)
    route = []
    for low in range(count):
        high = low | 1 << stride
        if high != low and high < count:
            route += [(low, high), (high, low)]
    return lax.ppermute(block, axis, route)


def extend_add(update, blocks):
    parent_blocks = (PIV + UPD) // BLOCK
    child_blocks = blocks.shape[0]
    onehot = (blocks[:, None] == jnp.arange(parent_blocks, dtype=jnp.int32)[None, :]).astype(
        jnp.float32
    )
    tile_grid = update.reshape(child_blocks, BLOCK, child_blocks, BLOCK)
    spread = jnp.einsum("ia,ixjy->axjy", onehot, tile_grid, precision=exact_mode)
    placed = jnp.einsum("axjy,jb->axby", spread, onehot, precision=exact_mode)
    return placed.reshape(parent_blocks * BLOCK, parent_blocks * BLOCK)


def exact_dot(left, right):
    return jnp.dot(left, right, precision=exact_mode, preferred_element_type=jnp.float32)


def inverse_factor(pivot_block):
    tile_count = PIV // BLOCK
    identity = jnp.eye(BLOCK, dtype=jnp.float32)
    remaining = pivot_block
    lower_tiles = {}
    diag_inverse = []
    for column_tile in range(tile_count):
        offset = column_tile * BLOCK
        diag_factor = jnp.linalg.cholesky(
            remaining[offset : offset + BLOCK, offset : offset + BLOCK]
        )
        tile_inverse = jax.scipy.linalg.solve_triangular(diag_factor, identity, lower=True)
        diag_inverse.append(tile_inverse)
        if column_tile + 1 < tile_count:
            below_rows = exact_dot(
                remaining[offset + BLOCK :, offset : offset + BLOCK], tile_inverse.T
            )
            for row_tile in range(column_tile + 1, tile_count):
                start_row = (row_tile - column_tile - 1) * BLOCK
                lower_tiles[row_tile, column_tile] = below_rows[start_row : start_row + BLOCK]
            trailing_part = remaining[offset + BLOCK :, offset + BLOCK :] - exact_dot(
                below_rows, below_rows.T
            )
            remaining = remaining.at[offset + BLOCK :, offset + BLOCK :].set(trailing_part)
    inverse_tiles = {}
    for column_tile in range(tile_count):
        inverse_tiles[column_tile, column_tile] = diag_inverse[column_tile]
        for row_tile in range(column_tile + 1, tile_count):
            accumulated = jnp.zeros((BLOCK, BLOCK), jnp.float32)
            for middle in range(column_tile, row_tile):
                accumulated = accumulated + exact_dot(
                    lower_tiles[row_tile, middle], inverse_tiles[middle, column_tile]
                )
            inverse_tiles[row_tile, column_tile] = -exact_dot(diag_inverse[row_tile], accumulated)
    zero_tile = jnp.zeros((BLOCK, BLOCK), jnp.float32)
    tile_rows = []
    for row_tile in range(tile_count):
        pieces = [
            inverse_tiles[row_tile, column_tile] if column_tile <= row_tile else zero_tile
            for column_tile in range(tile_count)
        ]
        tile_rows.append(jnp.concatenate(pieces, axis=1))
    return jnp.concatenate(tile_rows, axis=0)


def group_total(partial_value, level_index):
    portion = lax.psum_scatter(partial_value, "row", scatter_dimension=1, tiled=True)
    for bit_number in range(level_index):
        portion = portion + partner(portion, "leaf", bit_number)
    assembled = lax.all_gather(portion, "row", axis=1, tiled=True)
    return assembled


def body(panel0, panel1, panel2, panel3, maps1, maps2, maps3):
    panels = (panel0, panel1, panel2, panel3)
    block_maps = (maps1, maps1, maps2, maps3)
    row_devices = lax.axis_size("row")
    leaf_index = lax.axis_index("leaf")
    row_index = lax.axis_index("row")
    schur = jnp.zeros((UPD, UPD), jnp.float32)
    for level_index in range(4):
        group_leaves = 2**level_index
        position = leaf_index % group_leaves * row_devices + row_index
        group_devices = group_leaves * row_devices
        panel_rows = panels[level_index]
        row_count = panel_rows.shape[0]
        if level_index == 0:
            partial_value = jnp.zeros((PIV + UPD, PIV), jnp.float32)
            trailing = jnp.zeros((UPD, UPD), jnp.float32)
        else:
            child_front = leaf_index // (group_leaves // 2)
            blocks = lax.dynamic_index_in_dim(
                block_maps[level_index], child_front, 0, keepdims=False
            )
            upper = extend_add(schur, blocks)
            partial_value = upper[:, :PIV]
            trailing = upper[PIV:, PIV:]
        start = position * row_count
        current = lax.dynamic_slice_in_dim(partial_value, start, row_count, 0)
        partial_value = lax.dynamic_update_slice_in_dim(
            partial_value, current + panel_rows, start, 0
        )
        assembled = group_total(partial_value, level_index)
        inverse = inverse_factor(assembled[:PIV])
        column_count = PIV // group_devices
        picked = lax.dynamic_slice_in_dim(inverse, position * column_count, column_count, 0)
        columns = exact_dot(assembled[PIV:], picked.T)
        schur = trailing - exact_dot(columns, columns.T)
    sub_rows = UPD // (8 * row_devices)
    grouped = jnp.swapaxes(schur.reshape(8, row_devices, sub_rows, UPD), 0, 1)
    shared = lax.psum_scatter(grouped, "row", scatter_dimension=0, tiled=True)
    current = shared[0]
    for bit_number in (2, 1, 0):
        half_count = current.shape[0] // 2
        upper_side = leaf_index // 2**bit_number % 2
        lower_half = current[:half_count]
        upper_half = current[half_count:]
        kept_half = jnp.where(upper_side == 1, upper_half, lower_half)
        given_half = jnp.where(upper_side == 1, lower_half, upper_half)
        current = kept_half + partner(given_half, "leaf", bit_number)
    return current.reshape(sub_rows, UPD)


def solution(mesh):
    placed = (
        P(("leaf", "row"), None),
        P(("leaf", "row"), None),
        P(("leaf", "row"), None),
        P(("leaf", "row"), None),
        P(),
        P(),
        P(),
    )
    return jax.shard_map(
        body, mesh=mesh, in_specs=placed, out_specs=P(("leaf", "row"), None), check_vma=False
    )
```

profile of v0, /device:TPU:0, one launch (start us, length us, event | category | flops | bytes accessed | tf_op | source)
XLA Modules:
  0.0 1117.7 jit_solution(9129842647226602034)
XLA Ops:
  12.2 40.7 %reduce-scatter.8.cloned.1.call-done = f32[1536,128]{0,1:T(8,128)} async-done(((f32[1536,512]{0,1:T(8,128)}), f32[1536,128]{0,1:T(8,128)}) %reduce-scatter.8.cloned.1.call-update) | async-done | bytes 786448 | tf_op jit(solution)/shard_map/reduce_scatter | solution.py:86
  54.0 29.0 %all-gather.5.cloned.1.call-done = f32[1536,512]{0,1:T(8,128)} async-done(((f32[1536,128]{0,1:T(8,128)}), f32[1536,512]{0,1:T(8,128)}) %all-gather.5.cloned.1.call-update) | async-done | bytes 3145744 | tf_op jit(solution)/shard_map/all_gather | solution.py:89
  111.2 11.7 %cholesky.265 = f32[128,128]{1,0:T(8,128)S(1)} custom-call(f32[128,128]{1,0:T(8,128)S(1)} %fusion.202), custom_call_target="Cholesky" | custom-call | tf_op jit(solution)/shard_map/jit(cholesky)/cholesky | solution.py:48
  135.7 11.7 %cholesky.276 = f32[128,128]{1,0:T(8,128)S(1)} custom-call(f32[128,128]{1,0:T(8,128)S(1)} %fusion.200), custom_call_target="Cholesky" | custom-call | tf_op jit(solution)/shard_map/jit(cholesky)/cholesky | solution.py:48
  161.2 11.8 %cholesky.287 = f32[128,128]{1,0:T(8,128)S(1)} custom-call(f32[128,128]{1,0:T(8,128)S(1)} %fusion.198), custom_call_target="Cholesky" | custom-call | tf_op jit(solution)/shard_map/jit(cholesky)/cholesky | solution.py:48
  232.9 38.4 %reduce-scatter.10.cloned.1.call-done = f32[1536,128]{0,1:T(8,128)} async-done(((f32[1536,512]{0,1:T(8,128)}), f32[1536,128]{0,1:T(8,128)}) %reduce-scatter.10.cloned.1.call-update) | async-done | bytes 786448 | tf_op jit(solution)/shard_map/reduce_scatter | solution.py:86
  272.8 17.8 %collective-permute-done = f32[1536,128]{0,1:T(8,128)S(1)} collective-permute-done((f32[1536,128]{0,1:T(8,128)}, f32[1536,128]{0,1:T(8,128)S(1)}, u32[]{:S(2)}, u32[]{:S(2)}) %collective-permute-start) | collective-permute-done | bytes 786464 | tf_op jit(solution)/shard_map/ppermute | solution.py:21
  294.6 26.9 %all-gather.7.cloned.1.call-done = f32[1536,512]{0,1:T(8,128)} async-done(((f32[1536,128]{0,1:T(8,128)}), f32[1536,512]{0,1:T(8,128)}) %all-gather.7.cloned.1.call-update) | async-done | bytes 3145744 | tf_op jit(solution)/shard_map/all_gather | solution.py:89
  349.8 11.7 %cholesky.309 = f32[128,128]{1,0:T(8,128)S(1)} custom-call(f32[128,128]{1,0:T(8,128)S(1)} %fusion.194), custom_call_target="Cholesky" | custom-call | tf_op jit(solution)/shard_map/jit(cholesky)/cholesky | solution.py:48
  374.0 11.7 %cholesky.320 = f32[128,128]{1,0:T(8,128)S(1)} custom-call(f32[128,128]{1,0:T(8,128)S(1)} %fusion.192), custom_call_target="Cholesky" | custom-call | tf_op jit(solution)/shard_map/jit(cholesky)/cholesky | solution.py:48
  399.4 12.1 %cholesky.331 = f32[128,128]{1,0:T(8,128)S(1)} custom-call(f32[128,128]{1,0:T(8,128)S(1)} %fusion.190), custom_call_target="Cholesky" | custom-call | tf_op jit(solution)/shard_map/jit(cholesky)/cholesky | solution.py:48
  469.9 38.4 %reduce-scatter.12.cloned.1.call-done = f32[1536,128]{0,1:T(8,128)} async-done(((f32[1536,512]{0,1:T(8,128)}), f32[1536,128]{0,1:T(8,128)}) %reduce-scatter.12.cloned.1.call-update) | async-done | bytes 786448 | tf_op jit(solution)/shard_map/reduce_scatter | solution.py:86
  509.7 17.9 %collective-permute-done.1 = f32[1536,128]{0,1:T(8,128)S(1)} collective-permute-done((f32[1536,128]{0,1:T(8,128)}, f32[1536,128]{0,1:T(8,128)S(1)}, u32[]{:S(2)}, u32[]{:S(2)}) %collective-permute-start.1) | collective-permute-done | bytes 786464 | tf_op jit(solution)/shard_map/ppermute | solution.py:21
  530.4 16.8 %collective-permute-done.2 = f32[1536,128]{0,1:T(8,128)S(1)} collective-permute-done((f32[1536,128]{0,1:T(8,128)S(1)}, f32[1536,128]{0,1:T(8,128)S(1)}, u32[]{:S(2)}, u32[]{:S(2)}) %collective-permute-start.2) | collective-permute-done | bytes 786464 | tf_op jit(solution)/shard_map/ppermute | solution.py:21
  549.6 27.3 %all-gather.9.cloned.1.call-done = f32[1536,512]{0,1:T(8,128)} async-done(((f32[1536,128]{0,1:T(8,128)}), f32[1536,512]{0,1:T(8,128)}) %all-gather.9.cloned.1.call-update) | async-done | bytes 3145744 | tf_op jit(solution)/shard_map/all_gather | solution.py:89
  654.8 11.9 %cholesky.375 = f32[128,128]{1,0:T(8,128)S(1)} custom-call(f32[128,128]{1,0:T(8,128)S(1)} %fusion.182), custom_call_target="Cholesky" | custom-call | tf_op jit(solution)/shard_map/jit(cholesky)/cholesky | solution.py:48
  725.1 38.4 %reduce-scatter.14.cloned.1.call-done = f32[1536,128]{0,1:T(8,128)} async-done(((f32[1536,512]{0,1:T(8,128)}), f32[1536,128]{0,1:T(8,128)}) %reduce-scatter.14.cloned.1.call-update) | async-done | bytes 786448 | tf_op jit(solution)/shard_map/reduce_scatter | solution.py:86
  764.9 17.8 %collective-permute-done.3 = f32[1536,128]{0,1:T(8,128)S(1)} collective-permute-done((f32[1536,128]{0,1:T(8,128)}, f32[1536,128]{0,1:T(8,128)S(1)}, u32[]{:S(2)}, u32[]{:S(2)}) %collective-permute-start.3) | collective-permute-done | bytes 786464 | tf_op jit(solution)/shard_map/ppermute | solution.py:21
  785.6 16.7 %collective-permute-done.4 = f32[1536,128]{0,1:T(8,128)S(1)} collective-permute-done((f32[1536,128]{0,1:T(8,128)S(1)}, f32[1536,128]{0,1:T(8,128)S(1)}, u32[]{:S(2)}, u32[]{:S(2)}) %collective-permute-start.4) | collective-permute-done | bytes 786464 | tf_op jit(solution)/shard_map/ppermute | solution.py:21
  804.9 32.7 %collective-permute-done.5 = f32[1536,128]{0,1:T(8,128)S(1)} collective-permute-done((f32[1536,128]{0,1:T(8,128)S(1)}, f32[1536,128]{0,1:T(8,128)S(1)}, u32[]{:S(2)}, u32[]{:S(2)}) %collective-permute-start.5) | collective-permute-done | bytes 786464 | tf_op jit(solution)/shard_map/ppermute | solution.py:21
  838.9 28.4 %all-gather.11.cloned.1.call-done = f32[1536,512]{0,1:T(8,128)} async-done(((f32[1536,128]{0,1:T(8,128)}), f32[1536,512]{0,1:T(8,128)}) %all-gather.11.cloned.1.call-update) | async-done | bytes 3145744 | tf_op jit(solution)/shard_map/all_gather | solution.py:89
  945.8 11.9 %cholesky.419 = f32[128,128]{1,0:T(8,128)S(1)} custom-call(f32[128,128]{1,0:T(8,128)S(1)} %fusion.174), custom_call_target="Cholesky" | custom-call | tf_op jit(solution)/shard_map/jit(cholesky)/cholesky | solution.py:48
  982.2 84.4 %all-reduce.7.cloned.1.call-done = f32[4,8,32,1024]{3,2,0,1:T(8,128)} async-done(((f32[4,8,32,1024]{3,2,0,1:T(8,128)}), f32[4,8,32,1024]{3,2,0,1:T(8,128)}) %all-reduce.7.cloned.1.call-update) | async-done | bytes 4194320
  1072.9 23.1 %collective-permute-done.6 = f32[4,32,1024]{2,1,0:T(8,128)S(1)} collective-permute-done((f32[4,32,1024]{2,1,0:T(8,128)S(1)}, f32[4,32,1024]{2,1,0:T(8,128)S(1)}, u32[]{:S(2)}, u32[]{:S(2)}) %collective-permute-start.6) | collective-permute-done | bytes 524320 | tf_op jit(solution)/shard_map/ppermute | solution.py:21
  (340 shorter events, 513.2 us)
Async XLA Ops:
  6.5 47.5 %copy-start = (s32[8,8]{1,0:T(8,128)S(1)}, s32[8,8]{1,0:T(8,128)}, u32[]{:S(2)}) copy-start(s32[8,8]{1,0:T(8,128)} %param.38) | copy-start | bytes 772
  6.5 46.4 %reduce-scatter.8.cloned.1.call-start = ((), (), s32[]{:S(2)}) async-start(), calls=%async_computation.4 | async-start | bytes 3932160 | tf_op jit(solution)/shard_map/reduce_scatter | solution.py:86
  8.8 44.2 %copy-start.6 = (f32[192,512]{1,0:T(8,128)S(1)}, f32[192,512]{1,0:T(8,128)}, u32[]{:S(2)}) copy-start(f32[192,512]{1,0:T(8,128)} %param.35) | copy-start | bytes 1179652
  12.1 70.9 %all-gather.5.cloned.1.call-start = ((), (), s32[]{:S(2)}) async-start(), calls=%async_computation.5 | async-start | bytes 3932160 | tf_op jit(solution)/shard_map/all_gather | solution.py:89
  52.9 218.4 %reduce-scatter.10.cloned.1.call-start = ((), (), s32[]{:S(2)}) async-start(), calls=%async_computation.6 | async-start | bytes 3932160 | tf_op jit(solution)/shard_map/reduce_scatter | solution.py:86
  224.4 68.7 %copy-start.7 = (f32[96,512]{1,0:T(8,128)S(1)}, f32[96,512]{1,0:T(8,128)}, u32[]{:S(2)}) copy-start(f32[96,512]{1,0:T(8,128)} %param.36) | copy-start | bytes 589828
  232.9 88.6 %all-gather.7.cloned.1.call-start = ((), (), s32[]{:S(2)}) async-start(), calls=%async_computation.7 | async-start | bytes 3932160 | tf_op jit(solution)/shard_map/all_gather | solution.py:89
  271.3 19.3 %collective-permute-start = (f32[1536,128]{0,1:T(8,128)}, f32[1536,128]{0,1:T(8,128)S(1)}, u32[]{:S(2)}, u32[]{:S(2)}) collective-permute-start(f32[1536,128]{0,1:T(8,128)} %reduce-scatter.10.cloned.1.call-done), channel_id=1, source_target_pairs={{0,4},{4,0},{8,12},{12,8},{16,20},{20,16},{24,28},{28,24},{1,5},{5... | collective-permute-start | bytes 2359304 | tf_op jit(solution)/shard_map/ppermute | solution.py:21
  292.8 215.4 %reduce-scatter.12.cloned.1.call-start = ((), (), s32[]{:S(2)}) async-start(), calls=%async_computation.8 | async-start | bytes 3932160 | tf_op jit(solution)/shard_map/reduce_scatter | solution.py:86
  468.2 80.6 %copy-start.8 = (f32[48,512]{1,0:T(8,128)S(1)}, f32[48,512]{1,0:T(8,128)}, u32[]{:S(2)}) copy-start(f32[48,512]{1,0:T(8,128)} %param.37) | copy-start | bytes 294916
  468.2 81.4 %copy-start.9 = (s32[2,8]{1,0:T(2,128)S(1)}, s32[2,8]{1,0:T(2,128)}, u32[]{:S(2)}) copy-start(s32[2,8]{1,0:T(2,128)} %param.40) | copy-start | bytes 196
  469.8 107.1 %all-gather.9.cloned.1.call-start = ((), (), s32[]{:S(2)}) async-start(), calls=%async_computation.9 | async-start | bytes 3932160 | tf_op jit(solution)/shard_map/all_gather | solution.py:89
  508.3 19.3 %collective-permute-start.1 = (f32[1536,128]{0,1:T(8,128)}, f32[1536,128]{0,1:T(8,128)S(1)}, u32[]{:S(2)}, u32[]{:S(2)}) collective-permute-start(f32[1536,128]{0,1:T(8,128)} %reduce-scatter.12.cloned.1.call-done), channel_id=1, source_target_pairs={{0,4},{4,0},{8,12},{12,8},{16,20},{20,16},{24,28},{28,24},{1,5},{5... | collective-permute-start | bytes 2359304 | tf_op jit(solution)/shard_map/ppermute | solution.py:21
  528.9 18.3 %collective-permute-start.2 = (f32[1536,128]{0,1:T(8,128)S(1)}, f32[1536,128]{0,1:T(8,128)S(1)}, u32[]{:S(2)}, u32[]{:S(2)}) collective-permute-start(f32[1536,128]{0,1:T(8,128)S(1)} %add.230), channel_id=1, source_target_pairs={{0,8},{8,0},{4,12},{12,4},{16,24},{24,16},{20,28},{28,20},{1,9},{9... | collective-permute-start | bytes 2359304 | tf_op jit(solution)/shard_map/ppermute | solution.py:21
  548.2 215.2 %reduce-scatter.14.cloned.1.call-start = ((), (), s32[]{:S(2)}) async-start(), calls=%async_computation.10 | async-start | bytes 3932160 | tf_op jit(solution)/shard_map/reduce_scatter | solution.py:86
  725.0 142.4 %all-gather.11.cloned.1.call-start = ((), (), s32[]{:S(2)}) async-start(), calls=%async_computation.11 | async-start | bytes 3932160 | tf_op jit(solution)/shard_map/all_gather | solution.py:89
  763.4 19.3 %collective-permute-start.3 = (f32[1536,128]{0,1:T(8,128)}, f32[1536,128]{0,1:T(8,128)S(1)}, u32[]{:S(2)}, u32[]{:S(2)}) collective-permute-start(f32[1536,128]{0,1:T(8,128)} %reduce-scatter.14.cloned.1.call-done), channel_id=1, source_target_pairs={{0,4},{4,0},{8,12},{12,8},{16,20},{20,16},{24,28},{28,24},{1,5},{5... | collective-permute-start | bytes 2359304 | tf_op jit(solution)/shard_map/ppermute | solution.py:21
  784.0 18.3 %collective-permute-start.4 = (f32[1536,128]{0,1:T(8,128)S(1)}, f32[1536,128]{0,1:T(8,128)S(1)}, u32[]{:S(2)}, u32[]{:S(2)}) collective-permute-start(f32[1536,128]{0,1:T(8,128)S(1)} %add.241), channel_id=1, source_target_pairs={{0,8},{8,0},{4,12},{12,4},{16,24},{24,16},{20,28},{28,20},{1,9},{9... | collective-permute-start | bytes 2359304 | tf_op jit(solution)/shard_map/ppermute | solution.py:21
  802.4 35.2 %collective-permute-start.5 = (f32[1536,128]{0,1:T(8,128)S(1)}, f32[1536,128]{0,1:T(8,128)S(1)}, u32[]{:S(2)}, u32[]{:S(2)}) collective-permute-start(f32[1536,128]{0,1:T(8,128)S(1)} %add.242), channel_id=1, source_target_pairs={{0,16},{16,0},{4,20},{20,4},{8,24},{24,8},{12,28},{28,12},{1,17},{... | collective-permute-start | bytes 2359304 | tf_op jit(solution)/shard_map/ppermute | solution.py:21
  838.7 228.0 %all-reduce.7.cloned.1.call-start = ((), (), s32[]{:S(2)}) async-start(), calls=%async_computation.12 | async-start | bytes 8388608
  1066.6 44.3 %copy-start.1 = (s32[8,8]{1,0:T(8,128)S(1)}, s32[8,8]{1,0:T(8,128)}, u32[]{:S(2)}) copy-start(s32[8,8]{1,0:T(8,128)} %param.38) | copy-start | bytes 772
  1070.4 25.5 %collective-permute-start.6 = (f32[4,32,1024]{2,1,0:T(8,128)S(1)}, f32[4,32,1024]{2,1,0:T(8,128)S(1)}, u32[]{:S(2)}, u32[]{:S(2)}) collective-permute-start(f32[4,32,1024]{2,1,0:T(8,128)S(1)} %fusion.22), channel_id=1, source_target_pairs={{0,16},{16,0},{4,20},{20,4},{8,24},{24,8},{12,28},{28,12},{1,17},{... | collective-permute-start | bytes 1572872 | tf_op jit(solution)/shard_map/ppermute | solution.py:21
  1097.8 7.4 collective-permute-start.7
  1105.3 5.0 collective-permute-start.8
  (5 other events, 7.2 us)
Sparse Core Ops, SparseCore 0:
  12.3 40.5 reduce-scatter.7
  54.5 28.5 all-gather.4
  233.0 38.2 reduce-scatter.9
  293.0 28.5 all-gather.6
  469.9 38.2 reduce-scatter.11
  548.4 28.4 all-gather.8
  725.1 38.2 reduce-scatter.13
  838.8 28.5 all-gather.10
  981.1 85.4 all-reduce.6
where the time goes:
time: 1130 us; the launch traced here: 1120 us
  waiting for transfers between devices  505 us (45%)
  other arithmetic  388 us (34%)
  matrix products  115 us (10%)
  local copies, waits for them, and re-layouts  78.7 us (7%)
  starting transfers between devices  15.7 us (1%)
  between operations  15.2 us (1%)
    another operation x48, other arithmetic, inverse_factor(): jnp.linalg.cholesky(remaining[offset:offset + BLOCK, offset:offset + BLOCK])  199 us
    another operation x32, other arithmetic, inverse_factor(): jax.scipy.linalg.solve_triangular(diag_factor, identity, lower=True)  169 us
    reduce_scatter x4, waiting for transfers between devices, group_total(): lax.psum_scatter(partial_value, 'row', scatter_dimension=1, tiled=True)  156 us
    ppermute x9, waiting for transfers between devices, partner(): return lax.ppermute(block, axis, route)  153 us
    all_gather x4, waiting for transfers between devices, group_total(): assembled = lax.all_gather(portion, 'row', axis=1, tiled=True)  112 us
    unnamed x10, waiting for transfers between devices  84.6 us
    dot_general x96, matrix products, exact_dot(): jnp.dot(left, right, precision=exact_mode, preferred_element_type=jnp.flo...  72.2 us
    unnamed x36, local copies, waits for them, and re-layouts  47.8 us
  transfers between devices with their start and end apart: 18, of which 18 were waited for; matrix products, arithmetic and copies ran while one was open for 0% of the time, Pallas kernels for 0%

commit v1 on v0

v1 whole, which is shorter than its diff:
```python
import functools

import jax
import jax.numpy as jnp
from jax import lax
from jax.experimental import pallas as pl
from jax.experimental.pallas import tpu as pltpu
from jax.sharding import PartitionSpec as P

BLOCK = 128
SUB = 8
LEVELS = 4
CONTRACT_LAST = (((1,), (1,)), ((), ()))


def partner(block, axis, stride):
    count = lax.axis_size(axis)
    route = []
    for low in range(count):
        high = low | 1 << stride
        if high != low and high < count:
            route += [(low, high), (high, low)]
    return lax.ppermute(block, axis, route)


def halves(value):
    high = value.astype(jnp.bfloat16)
    low = (value - high.astype(jnp.float32)).astype(jnp.bfloat16)
    return high, low


def dot_split(left, right):
    left_high, left_low = left
    right_high, right_low = right

    def one(a, b):
        return lax.dot_general(a, b, CONTRACT_LAST, preferred_element_type=jnp.float32)

    return one(left_high, right_high) + (one(left_high, right_low) + one(left_low, right_high))


def dot_nt(left, right):
    return dot_split(halves(left), halves(right))


def spread(value, rows, columns):
    return jnp.broadcast_to(value, (rows, columns))


def diagonal_inverse(block):
    count = BLOCK // SUB
    rows = [block[v * SUB : (v + 1) * SUB] for v in range(count)]
    lane = lax.broadcasted_iota(jnp.int32, (SUB, BLOCK), 1)
    sub = lax.broadcasted_iota(jnp.int32, (SUB, BLOCK), 0)
    for b in range(count):
        base = b * SUB
        inside = (lane >= base) & (lane < base + SUB)
        own = rows[b]
        columns = [spread(own[:, base + j : base + j + 1], SUB, BLOCK) for j in range(SUB)]
        a = [
            [spread(columns[j][i : i + 1], SUB, BLOCK) for j in range(i + 1)] for i in range(SUB)
        ]
        inverse = []
        ratio = [[None] * SUB for _ in range(SUB)]
        for i in range(SUB):
            inverse.append(1.0 / a[i][i])
            for j in range(i + 1, SUB):
                ratio[j][i] = a[j][i] * inverse[i]
            for j in range(i + 1, SUB):
                for k in range(i + 1, j + 1):
                    a[j][k] = a[j][k] - ratio[j][i] * a[k][i]
        cleared = jnp.where(inside, 0.0, own)
        pivots = []
        for j in range(SUB):
            row = spread(cleared[j : j + 1], SUB, BLOCK)
            row = jnp.where(lane == base + j, 1.0, row)
            for i in range(j):
                row = row - ratio[j][i] * pivots[i]
            pivots.append(row)
        for v in range(b + 1, count):
            old = rows[v]
            new = jnp.where(inside, 0.0, old)
            factors = []
            for j in range(SUB):
                column = spread(old[:, base + j : base + j + 1], SUB, BLOCK)
                for i in range(j):
                    column = column - factors[i] * a[j][i]
                factors.append(column * inverse[j])
            for j in range(SUB):
                new = new - factors[j] * pivots[j]
            rows[v] = new
        final = jnp.zeros((SUB, BLOCK), jnp.float32)
        scale = jnp.ones((SUB, BLOCK), jnp.float32)
        for j in range(SUB):
            final = jnp.where(sub == j, pivots[j], final)
            scale = jnp.where(sub == j, a[j][j], scale)
        rows[b] = jnp.where(lane <= sub + base, final / jnp.sqrt(scale), 0.0)
    return jnp.concatenate(rows, axis=0)


def factor(work, out):
    order = work.shape[0]
    tiles = order // BLOCK
    row_ids = lax.broadcasted_iota(jnp.int32, (order, BLOCK), 0)

    def step(j, carry):
        start = pl.multiple_of(j * BLOCK, BLOCK)
        span = pl.ds(start, BLOCK)
        inverse = diagonal_inverse(work[span, span])
        below = jnp.where(row_ids >= start + BLOCK, work[:, span], 0.0)
        column = dot_nt(below, inverse)
        out[:, span] = column
        out[span, span] = inverse
        pieces = halves(column)
        work[...] = work[...] - dot_split(pieces, pieces)
        return carry

    lax.fori_loop(0, tiles, step, 0)


def solve_below(factors, columns):
    order = factors.shape[0]
    for j in range(order // BLOCK):
        span = slice(j * BLOCK, (j + 1) * BLOCK)
        value = columns[:, span]
        if j:
            value = value - dot_nt(columns[:, : j * BLOCK], factors[span, : j * BLOCK])
        columns[:, span] = dot_nt(value, factors[span, span])


def front_kernel(level, row_count, *refs):
    last = level == LEVELS - 1
    group = 2**level
    if level == 0:
        info, inverse_map, gathered, *rest = refs
        old = None
    else:
        info, inverse_map, gathered, old, *rest = refs
    if last:
        out, work, factors, columns = rest
    else:
        if level == LEVELS - 2:
            kept, share, extra, work, factors, columns, placed = rest
        else:
            kept, share, work, factors, columns, placed = rest
    front, order = gathered.shape
    chunk = front // (row_count * group)
    below = front - order
    for member in range(group):
        for r in range(row_count):
            source = (r * group + member) * chunk
            target = (member * row_count + r) * chunk
            first = max(0, min(chunk, order - target))
            if first:
                work[target : target + first] = gathered[source : source + first]
            if first < chunk:
                low = target + first - order
                columns[low : low + chunk - first] = gathered[source + first : source + chunk]
    factor(work, factors)
    solve_below(factors, columns)
    if last:
        rows = out.shape[0]
        position = info[0] * row_count + info[1]
        mine = columns[pl.ds(pl.multiple_of(position * rows, 8), rows)]
        out[...] = dot_nt(mine, columns[...])
        return
    depth = 0 if old is None else old.shape[1]
    width = order // group
    if old is not None:
        kept[:below, :depth] = old[:below]
    offset = pl.multiple_of(info[0] % group * width, BLOCK)
    kept[:below, depth:] = columns[:, pl.ds(offset, width)]
    kept[below:] = jnp.zeros((BLOCK, depth + width), jnp.float32)
    for i in range(front // BLOCK):
        block = pl.multiple_of(inverse_map[i] * BLOCK, BLOCK)
        placed[i * BLOCK : (i + 1) * BLOCK] = kept[pl.ds(block, BLOCK)]
    pivots = halves(placed[:order])
    small = chunk // 2
    for member in range(2 * group):
        start = pl.multiple_of((member * row_count + info[1]) * small, 8)
        piece = halves(placed[pl.ds(start, small)])
        share[member * small : (member + 1) * small] = -dot_split(piece, pivots)
    kept[:below] = placed[order:]
    if level == LEVELS - 2:
        top = 2 * group
        rows = below // (top * row_count)
        full = halves(placed[order:])
        for member in range(top):
            start = pl.multiple_of(order + (member * row_count + info[1]) * rows, 8)
            piece = halves(placed[pl.ds(start, rows)])
            extra[member * rows : (member + 1) * rows] = -dot_split(piece, full)


def front_step(level, info, inverse_map, gathered, old, row_count):
    front, order = gathered.shape
    below = front - order
    depth = 0 if old is None else old.shape[1]
    width = order // 2**level
    float32 = jnp.float32
    scratch = [
        pltpu.VMEM((order, order), float32),
        pltpu.VMEM((order, order), float32),
        pltpu.VMEM((below, order), float32),
    ]
    if level == LEVELS - 1:
        rows = below // (2**level * row_count)
        shapes = jax.ShapeDtypeStruct((rows, below), float32)
    else:
        shapes = [
            jax.ShapeDtypeStruct((below + BLOCK, depth + width), float32),
            jax.ShapeDtypeStruct((front // row_count, order), float32),
        ]
        scratch.append(pltpu.VMEM((front, depth + width), float32))
        if level == LEVELS - 2:
            shapes.append(jax.ShapeDtypeStruct((below // row_count, below), float32))
    operands = [info, inverse_map, gathered]
    specs = [pl.BlockSpec(memory_space=pltpu.SMEM)] * 2 + [pl.BlockSpec(memory_space=pltpu.VMEM)]
    if old is not None:
        operands.append(old)
        specs.append(pl.BlockSpec(memory_space=pltpu.VMEM))
    return pl.pallas_call(
        functools.partial(front_kernel, level, row_count),
        out_shape=shapes,
        in_specs=specs,
        scratch_shapes=scratch,
        name=f"front{level}",
        compiler_params=pltpu.CompilerParams(vmem_limit_bytes=60 * 2**20),
    )(*operands)


def body(panel0, panel1, panel2, panel3, maps1, maps2, maps3):
    panels = (panel0, panel1, panel2, panel3)
    block_maps = (maps1, maps2, maps3)
    row_count = lax.axis_size("row")
    leaf = lax.axis_index("leaf")
    row = lax.axis_index("row")
    order = panel0.shape[1]
    front = panel0.shape[0] * row_count
    parents = front // BLOCK
    children = (front - order) // BLOCK
    old = None
    share = panel0
    extra = None
    for level in range(LEVELS):
        group = 2**level
        member = leaf % group
        if level:
            rows = panels[level].shape[0]
            start = member * rows
            mine = lax.dynamic_slice_in_dim(share, start, rows, 0) + panels[level]
            share = lax.dynamic_update_slice_in_dim(share, mine, start, 0)
            for bit in range(level):
                share = share + partner(share, "leaf", bit)
        gathered = lax.all_gather(share, "row", axis=0, tiled=True)
        info = jnp.stack([member, row]).astype(jnp.int32)
        if level < LEVELS - 1:
            blocks = lax.dynamic_index_in_dim(block_maps[level], leaf // group, 0, keepdims=False)
            hit = blocks[None, :] == jnp.arange(parents, dtype=jnp.int32)[:, None]
            back = jnp.min(
                jnp.where(hit, jnp.arange(children, dtype=jnp.int32)[None, :], children), axis=1
            )
        else:
            back = jnp.zeros((parents,), jnp.int32)
        result = front_step(level, info, back, gathered, old, row_count)
        if level == LEVELS - 1:
            product = result
        elif level == LEVELS - 2:
            old, share, extra = result
        else:
            old, share = result
    current = extra.reshape(2 ** (LEVELS - 1), -1, extra.shape[1])
    for bit in reversed(range(LEVELS - 1)):
        half = current.shape[0] // 2
        upper = leaf // 2**bit % 2
        kept = lax.dynamic_slice_in_dim(current, upper * half, half, 0)
        given = lax.dynamic_slice_in_dim(current, (1 - upper) * half, half, 0)
        current = kept + partner(given, "leaf", bit)
    return current[0] - product


def solution(mesh):
    rows = P(("leaf", "row"), None)
    return jax.shard_map(
        body,
        mesh=mesh,
        in_specs=(rows, rows, rows, rows, P(), P(), P()),
        out_specs=rows,
        check_vma=False,
    )
```

time: 1130 us -> 439 us (0.39)
  other arithmetic: 388 us -> 18 us
  waiting for transfers between devices: 505 us -> 241 us
  Pallas kernels: 0 us -> 146 us
  matrix products: 115 us -> 0 us
  local copies, waits for them, and re-layouts: 78.7 us -> 1.35 us
    another operation x80 -> x4, other arithmetic: 368 us -> 2.35 us  [body(): info = jnp.stack([member, row]).astype(jnp.int32)]
    reduce_scatter x4 -> x0, waiting for transfers between devices: 156 us -> none  [group_total(): lax.psum_scatter(partial_value, 'row', scatter_dimension=1, tiled=True)]
    pallas_call x0 -> x4, Pallas kernels: none -> 146 us  [front_step(): pl.pallas_call(functools.partial(front_kernel, level, row_count), out_sha...]
    dot_general x102 -> x0, matrix products: 110 us -> none  [the longest x96 72.2 us: exact_dot(): jnp.dot(left, right, precision=exact_mode, preferred_element_type=jnp.flo...]
    unnamed x10 -> x4, waiting for transfers between devices: 84.6 us -> 0.76 us
    unnamed x36 -> x12, local copies, waits for them, and re-layouts: 47.8 us -> 0.02 us
    all_gather x4, waiting for transfers between devices: 112 us -> 85.4 us  [body(): gathered = lax.all_gather(share, 'row', axis=0, tiled=True)]
    slice x27 -> x0, local copies, waits for them, and re-layouts: 15.9 us -> none  [the longest x3 11.5 us: body(): partial_value = upper[:, :PIV]]
  transfers between devices with their start and end apart: 18 -> 13, of which waited for: 18 -> 11; matrix products, arithmetic and copies ran while one was open for 0% -> 1% of each run, Pallas kernels for 0% -> 7%
where the time goes in v1:
time: 439 us; the launch traced here: 432 us
  waiting for transfers between devices  241 us (55%)
  Pallas kernels  146 us (33%)
  other arithmetic  18 us (4%)
  between operations  13.6 us (3%)
  starting transfers between devices  12 us (3%)
    ppermute x9, waiting for transfers between devices, partner(): return lax.ppermute(block, axis, route)  155 us
    pallas_call x4, Pallas kernels, front_step(): pl.pallas_call(functools.partial(front_kernel, level, row_count), out_sha...  146 us
    all_gather x4, waiting for transfers between devices, body(): gathered = lax.all_gather(share, 'row', axis=0, tiled=True)  85.4 us
    ppermute x9, starting transfers between devices, partner(): return lax.ppermute(block, axis, route)  11.7 us
  transfers between devices with their start and end apart: 13, of which 11 were waited for; matrix products, arithmetic and copies ran while one was open for 1% of the time, Pallas kernels for 7%

profile of v1, /device:TPU:0, one launch (start us, length us, event | category | flops | bytes accessed | tf_op | source)
XLA Modules:
  0.0 431.9 jit_solution(12919952110922277667)
XLA Ops:
  8.6 31.6 %all-gather.5.cloned.1.call-done.refs_2_ = f32[1536,512]{1,0:T(8,128)} async-done(((f32[384,512]{1,0:T(8,128)}), f32[1536,512]{1,0:T(8,128)}) %all-gather.5.cloned.1.call-update) | async-done | bytes 3145744 | tf_op jit(solution)/shard_map/all_gather | solution.py:254
  40.2 30.3 %front0.1 = (f32[1152,512]{1,0:T(8,128)}, f32[384,512]{1,0:T(8,128)}) custom-call(s32[2]{0:T(128)} %pad_add_fusion.2.refs_0_, s32[12]{0:T(128)} %select_reduce_fusion.refs_1_, f32[1536,512]{1,0:T(8,128)} %all-gather.5.cloned.1.call-done.refs_2_), custom_call_target="tpu_custom_call" | custom-call | tf_op jit(solution)/shard_map/front0/pallas_call | solution.py:221
  70.4 1.8 add_dynamic-update-slice_fusion
  73.7 18.4 %collective-permute-done = f32[384,512]{1,0:T(8,128)S(1)} collective-permute-done((f32[384,512]{1,0:T(8,128)}, f32[384,512]{1,0:T(8,128)S(1)}, u32[]{:S(2)}, u32[]{:S(2)}) %collective-permute-start) | collective-permute-done | bytes 786464 | tf_op jit(solution)/shard_map/ppermute | solution.py:23
  92.1 2.2 add.107
  96.5 26.5 %all-gather.7.cloned.1.call-done.refs_2_ = f32[1536,512]{1,0:T(8,128)} async-done(((f32[384,512]{1,0:T(8,128)}), f32[1536,512]{1,0:T(8,128)}) %all-gather.7.cloned.1.call-update) | async-done | bytes 3145744 | tf_op jit(solution)/shard_map/all_gather | solution.py:254
  123.0 33.1 %front1.1 = (f32[1152,768]{1,0:T(8,128)}, f32[384,512]{1,0:T(8,128)}) custom-call(s32[2]{0:T(128)} %pad_add_fusion.1.refs_0_, s32[12]{0:T(128)} %select_reduce_fusion.1.refs_1_, f32[1536,512]{1,0:T(8,128)} %all-gather.7.cloned.1.call-done.refs_2_, f32[1152,512]{1,0:T(8,128)} %get-tuple-element.13.refs_3_), custom_call_target="tpu_custom_call" | custom-call | tf_op jit(solution)/shard_map/front1/pallas_call | solution.py:221
  156.2 1.6 add_dynamic-update-slice_fusion.1
  159.3 18.4 %collective-permute-done.1 = f32[384,512]{1,0:T(8,128)S(1)} collective-permute-done((f32[384,512]{1,0:T(8,128)}, f32[384,512]{1,0:T(8,128)S(1)}, u32[]{:S(2)}, u32[]{:S(2)}) %collective-permute-start.1) | collective-permute-done | bytes 786464 | tf_op jit(solution)/shard_map/ppermute | solution.py:23
  179.0 1.6 collective-permute-start.2
  180.6 17.3 %collective-permute-done.2 = f32[384,512]{1,0:T(8,128)S(1)} collective-permute-done((f32[384,512]{1,0:T(8,128)S(1)}, f32[384,512]{1,0:T(8,128)S(1)}, u32[]{:S(2)}, u32[]{:S(2)}) %collective-permute-start.2) | collective-permute-done | bytes 786464 | tf_op jit(solution)/shard_map/ppermute | solution.py:23
  200.3 27.3 %all-gather.9.cloned.1.call-done.refs_2_ = f32[1536,512]{1,0:T(8,128)} async-done(((f32[384,512]{1,0:T(8,128)}), f32[1536,512]{1,0:T(8,128)}) %all-gather.9.cloned.1.call-update) | async-done | bytes 3145744 | tf_op jit(solution)/shard_map/all_gather | solution.py:254
  227.6 51.6 %front2.1 = (f32[1152,896]{1,0:T(8,128)}, f32[384,512]{1,0:T(8,128)}, f32[256,1024]{1,0:T(8,128)}) custom-call(s32[2]{0:T(128)} %pad_add_fusion.refs_0_, s32[12]{0:T(128)} %select_reduce_fusion.2.refs_1_, f32[1536,512]{1,0:T(8,128)} %all-gather.9.cloned.1.call-done.refs_2_, f32[1152,768]{1,0:T(8,128)} %get-tuple-element.15.refs_3_), custom_call_target="tpu_custom_call" | custom-call | tf_op jit(solution)/shard_map/front2/pallas_call | solution.py:221
  279.2 1.5 add_dynamic-update-slice_fusion.2
  282.2 18.4 %collective-permute-done.6 = f32[384,512]{1,0:T(8,128)S(1)} collective-permute-done((f32[384,512]{1,0:T(8,128)}, f32[384,512]{1,0:T(8,128)S(1)}, u32[]{:S(2)}, u32[]{:S(2)}) %collective-permute-start.6) | collective-permute-done | bytes 786464 | tf_op jit(solution)/shard_map/ppermute | solution.py:23
  302.0 1.6 collective-permute-start.7
  303.5 17.3 %collective-permute-done.7 = f32[384,512]{1,0:T(8,128)S(1)} collective-permute-done((f32[384,512]{1,0:T(8,128)S(1)}, f32[384,512]{1,0:T(8,128)S(1)}, u32[]{:S(2)}, u32[]{:S(2)}) %collective-permute-start.7) | collective-permute-done | bytes 786464 | tf_op jit(solution)/shard_map/ppermute | solution.py:23
  321.0 2.5 collective-permute-start.8
  323.5 33.3 %collective-permute-done.8 = f32[384,512]{1,0:T(8,128)S(1)} collective-permute-done((f32[384,512]{1,0:T(8,128)S(1)}, f32[384,512]{1,0:T(8,128)S(1)}, u32[]{:S(2)}, u32[]{:S(2)}) %collective-permute-start.8) | collective-permute-done | bytes 786464 | tf_op jit(solution)/shard_map/ppermute | solution.py:23
  358.0 25.0 %collective-permute-done.3 = f32[4,32,1024]{2,1,0:T(8,128)S(1)} collective-permute-done((f32[4,32,1024]{2,1,0:T(8,128)S(1)}, f32[4,32,1024]{2,1,0:T(8,128)S(1)}, u32[]{:S(2)}, u32[]{:S(2)}) %collective-permute-start.3) | collective-permute-done | bytes 524320 | tf_op jit(solution)/shard_map/ppermute | solution.py:23
  383.3 6.6 %collective-permute-done.4 = f32[2,32,1024]{2,1,0:T(8,128)S(1)} collective-permute-done((f32[2,32,1024]{2,1,0:T(8,128)S(1)}, f32[2,32,1024]{2,1,0:T(8,128)S(1)}, u32[]{:S(2)}, u32[]{:S(2)}) %collective-permute-start.4) | collective-permute-done | bytes 262176 | tf_op jit(solution)/shard_map/ppermute | solution.py:23
  389.9 1.5 collective-permute-start.5
  392.6 31.0 %front3.1 = f32[32,1024]{1,0:T(8,128)} custom-call(s32[2]{0:T(128)} %pad_add_fusion.3.refs_0_, s32[12]{0:T(128)} %broadcast_1_refs_1_.2.refs_1_, f32[1536,512]{1,0:T(8,128)} %all-gather.11.cloned.1.call-done.refs_2_, f32[1152,896]{1,0:T(8,128)} %get-tuple-element.18.refs_3_), custom_call_target="tpu_custom_call" | custom-call | tf_op jit(solution)/shard_map/front3/pallas_call | solution.py:221
  423.6 1.6 bitcast_subtract_fusion
  (48 shorter events, 16.2 us)
Async XLA Ops:
  6.5 0.8 copy-start
  6.5 63.9 %copy-start.2 = (f32[192,512]{1,0:T(8,128)S(1)}, f32[192,512]{1,0:T(8,128)}, u32[]{:S(2)}) copy-start(f32[192,512]{1,0:T(8,128)} %param.8) | copy-start | bytes 1179652
  6.5 33.6 %all-gather.5.cloned.1.call-start = ((), (), s32[]{:S(2)}) async-start(), calls=%async_computation | async-start | bytes 3932160 | tf_op jit(solution)/shard_map/all_gather | solution.py:254
  7.3 115.8 %all-gather.7.cloned.1.call-start = ((), (), s32[]{:S(2)}) async-start(), calls=%async_computation.1 | async-start | bytes 3932160 | tf_op jit(solution)/shard_map/all_gather | solution.py:254
  72.3 19.9 %collective-permute-start = (f32[384,512]{1,0:T(8,128)}, f32[384,512]{1,0:T(8,128)S(1)}, u32[]{:S(2)}, u32[]{:S(2)}) collective-permute-start(f32[384,512]{1,0:T(8,128)} %add_dynamic-update-slice_fusion), channel_id=1, source_target_pairs={{0,4},{4,0},{8,12},{12,8},{16,20},{20,16},{24,28},{28,24},{1,5},{5... | collective-permute-start | bytes 2359304 | tf_op jit(solution)/shard_map/ppermute | solution.py:23
  94.3 61.8 %copy-start.3 = (f32[96,512]{1,0:T(8,128)S(1)}, f32[96,512]{1,0:T(8,128)}, u32[]{:S(2)}) copy-start(f32[96,512]{1,0:T(8,128)} %param.9) | copy-start | bytes 589828
  94.4 133.3 %all-gather.9.cloned.1.call-start = ((), (), s32[]{:S(2)}) async-start(), calls=%async_computation.2 | async-start | bytes 3932160 | tf_op jit(solution)/shard_map/all_gather | solution.py:254
  156.1 43.5 %copy-start.5 = (s32[2,8]{1,0:T(2,128)S(1)}, s32[2,8]{1,0:T(2,128)}, u32[]{:S(2)}) copy-start(s32[2,8]{1,0:T(2,128)} %param.13) | copy-start | bytes 196
  157.8 19.9 %collective-permute-start.1 = (f32[384,512]{1,0:T(8,128)}, f32[384,512]{1,0:T(8,128)S(1)}, u32[]{:S(2)}, u32[]{:S(2)}) collective-permute-start(f32[384,512]{1,0:T(8,128)} %add_dynamic-update-slice_fusion.1), channel_id=1, source_target_pairs={{0,4},{4,0},{8,12},{12,8},{16,20},{20,16},{24,28},{28,24},{1,5},{5... | collective-permute-start | bytes 2359304 | tf_op jit(solution)/shard_map/ppermute | solution.py:23
  179.0 18.9 %collective-permute-start.2 = (f32[384,512]{1,0:T(8,128)S(1)}, f32[384,512]{1,0:T(8,128)S(1)}, u32[]{:S(2)}, u32[]{:S(2)}) collective-permute-start(f32[384,512]{1,0:T(8,128)S(1)} %add.110), channel_id=1, source_target_pairs={{0,8},{8,0},{4,12},{12,4},{16,24},{24,16},{20,28},{28,20},{1,9},{9... | collective-permute-start | bytes 2359304 | tf_op jit(solution)/shard_map/ppermute | solution.py:23
  199.0 193.1 %all-gather.11.cloned.1.call-start = ((), (), s32[]{:S(2)}) async-start(), calls=%async_computation.3 | async-start | bytes 3932160 | tf_op jit(solution)/shard_map/all_gather | solution.py:254
  227.6 51.6 %copy-start.4 = (f32[48,512]{1,0:T(8,128)S(1)}, f32[48,512]{1,0:T(8,128)}, u32[]{:S(2)}) copy-start(f32[48,512]{1,0:T(8,128)} %param.10) | copy-start | bytes 294916
  280.8 19.9 %collective-permute-start.6 = (f32[384,512]{1,0:T(8,128)}, f32[384,512]{1,0:T(8,128)S(1)}, u32[]{:S(2)}, u32[]{:S(2)}) collective-permute-start(f32[384,512]{1,0:T(8,128)} %add_dynamic-update-slice_fusion.2), channel_id=1, source_target_pairs={{0,4},{4,0},{8,12},{12,8},{16,20},{20,16},{24,28},{28,24},{1,5},{5... | collective-permute-start | bytes 2359304 | tf_op jit(solution)/shard_map/ppermute | solution.py:23
  302.0 55.9 %copy-start.1 = (f32[256,1024]{1,0:T(8,128)S(1)}, f32[256,1024]{1,0:T(8,128)}, u32[]{:S(2)}) copy-start(f32[256,1024]{1,0:T(8,128)} %get-tuple-element.16) | copy-start | bytes 3145732
  302.0 18.9 %collective-permute-start.7 = (f32[384,512]{1,0:T(8,128)S(1)}, f32[384,512]{1,0:T(8,128)S(1)}, u32[]{:S(2)}, u32[]{:S(2)}) collective-permute-start(f32[384,512]{1,0:T(8,128)S(1)} %add.126), channel_id=1, source_target_pairs={{0,8},{8,0},{4,12},{12,4},{16,24},{24,16},{20,28},{28,20},{1,9},{9... | collective-permute-start | bytes 2359304 | tf_op jit(solution)/shard_map/ppermute | solution.py:23
  321.0 35.8 %collective-permute-start.8 = (f32[384,512]{1,0:T(8,128)S(1)}, f32[384,512]{1,0:T(8,128)S(1)}, u32[]{:S(2)}, u32[]{:S(2)}) collective-permute-start(f32[384,512]{1,0:T(8,128)S(1)} %add.127), channel_id=1, source_target_pairs={{0,16},{16,0},{4,20},{20,4},{8,24},{24,8},{12,28},{28,12},{1,17},{... | collective-permute-start | bytes 2359304 | tf_op jit(solution)/shard_map/ppermute | solution.py:23
  357.9 25.1 %collective-permute-start.3 = (f32[4,32,1024]{2,1,0:T(8,128)S(1)}, f32[4,32,1024]{2,1,0:T(8,128)S(1)}, u32[]{:S(2)}, u32[]{:S(2)}) collective-permute-start(f32[4,32,1024]{2,1,0:T(8,128)S(1)} %constant_dynamic-slice_fusion.2), channel_id=1, source_target_pairs={{0,16},{16,0},{4,20},{20,4},{8,24},{24,8},{12,28},{28,12},{1,17},{... | collective-permute-start | bytes 1572872 | tf_op jit(solution)/shard_map/ppermute | solution.py:23
  383.2 6.7 %collective-permute-start.4 = (f32[2,32,1024]{2,1,0:T(8,128)S(1)}, f32[2,32,1024]{2,1,0:T(8,128)S(1)}, u32[]{:S(2)}, u32[]{:S(2)}) collective-permute-start(f32[2,32,1024]{2,1,0:T(8,128)S(1)} %constant_dynamic-slice_fusion.1), channel_id=1, source_target_pairs={{0,8},{8,0},{4,12},{12,4},{16,24},{24,16},{20,28},{28,20},{1,9},{9... | collective-permute-start | bytes 786440 | tf_op jit(solution)/shard_map/ppermute | solution.py:23
  389.9 33.7 %collective-permute-start.5 = (f32[1,32,1024]{2,1,0:T(8,128)S(1)}, f32[1,32,1024]{2,1,0:T(8,128)S(1)}, u32[]{:S(2)}, u32[]{:S(2)}) collective-permute-start(f32[1,32,1024]{2,1,0:T(8,128)S(1)} %constant_dynamic-slice_fusion), channel_id=1, source_target_pairs={{0,4},{4,0},{8,12},{12,8},{16,20},{20,16},{24,28},{28,24},{1,5},{5... | collective-permute-start | bytes 393224 | tf_op jit(solution)/shard_map/ppermute | solution.py:23
Sparse Core Ops, SparseCore 0:
  8.9 31.2 all-gather.4
  94.5 28.4 all-gather.6
  199.1 28.4 all-gather.8
  358.0 28.4 all-gather.10
